TPU v7x, 32 devices: a whole 2x2x4 slice. The times are simulated.
32 devices in a mesh: occ: 4 (over z), vir: 8 (over y, x, core).
Axes of the slice: x: 2, y: 2, z: 4, core: 2. Of those that a mesh axis runs over, the one named last changes fastest.
Arguments:
- amplitudes: float32 [64, 1441792], P(None, ('occ', 'vir')), may hold values from -6 to 6
- slab: float32 [128, 1441792], P(None, ('occ', 'vir')), may hold values from -0.0048828125 to 0.0048828125
- mirror: int32 [128], replicated, may hold values from 0 to 127, as said below
Outputs:
- ladder: float32 [64, 128], P('occ')
Inputs may be any that keep to these rules, and one draw needn't show every extreme that they name: mirror pairs the rows: mirror[mirror[m]] = m and mirror[m] != m for every m.
All inputs are finite; a program needn't handle non-finite values.
Results may differ from a plain program's by a relative error of at most 0.000086.
Values sent between devices are 32-bit elements; how exact they have to be, the bound alone decides.
A program may use at most 128 MiB of HBM per device.

v0:
```python
import jax
import jax.numpy as jnp
from jax import lax
from jax.sharding import PartitionSpec as P


def contract(left, right):
    return lax.dot_general(
        left,
        right,
        (((1,), (1,)), ((), ())),
        precision=lax.Precision.HIGHEST,
        preferred_element_type=jnp.float32,
    )


def per_device(amplitudes, slab, mirror):
    own_rows = amplitudes.shape[0] // lax.axis_size("occ")
    partial_sum = contract(amplitudes, slab)
    summed = lax.psum(partial_sum, ("occ", "vir"))
    totals = lax.dynamic_slice_in_dim(summed, lax.axis_index("occ") * own_rows, own_rows, 0)
    return totals - jnp.take(totals, mirror, axis=1)


def solution(mesh):
    placed = (P(None, ("occ", "vir")), P(None, ("occ", "vir")), P())
    return jax.shard_map(
        per_device, mesh=mesh, in_specs=placed, out_specs=P("occ", None), check_vma=False
    )
```

profile of v0, /device:TPU:0, one launch (start us, length us, event | category | flops | bytes accessed | tf_op | source)
XLA Modules:
  0.0 71.5 jit_solution(2949817621040517710)
XLA Ops:
  0.0 0.0 copy-start
  0.0 27.9 %fusion = f32[64,128]{1,0:T(8,128)S(1)} fusion(f32[64,45056]{1,0:T(8,128)} %param.3, f32[128,45056]{1,0:T(8,128)} %param.4), kind=kOutput, calls=%fused_computation.6 | convolution fusion | flops 4429185024 | bytes 34635776 | tf_op jit(solution)/shard_map/dot_general | solution.py:8
  27.9 42.1 %psum.7 = f32[64,128]{1,0:T(8,128)S(1)} all-reduce(f32[64,128]{1,0:T(8,128)S(1)} %fusion), channel_id=1, replica_groups=mesh['occ'=4,'vir'=8] {'occ','vir'}, use_global_device_ids=true, to_apply=%region_0.0 | all-reduce | flops 8192 | bytes 65536 | tf_op jit(solution)/shard_map/psum | solution.py:20
  70.0 0.1 copy.4
  70.1 0.0 copy-done
  70.2 0.6 gather_fusion
  70.9 0.6 bitcast_subtract_fusion
  (5 shorter events, 0.1 us)
Async XLA Ops:
  0.0 70.1 %copy-start = (s32[128]{0:T(128)S(1)}, s32[128]{0:T(128)}, u32[]{:S(2)}) copy-start(s32[128]{0:T(128)} %param.5) | copy-start | bytes 1540
where the time goes:
time: 71.7 us; the launch traced here: 71.5 us
  blocking collectives  42.1 us (59%)
  matrix products  27.9 us (39%)
  local copies, waits for them, and re-layouts  0.81 us (1%)
    psum x1, blocking collectives, per_device(): summed = lax.psum(partial_sum, ('occ', 'vir'))  42.1 us
    dot_general x1, matrix products, contract(): lax.dot_general(left, right, (((1,), (1,)), ((), ())), precision=lax.Prec...  27.9 us

commit v1 on v0

v1 whole, which is shorter than its diff:
```python
import functools

import jax
import jax.numpy as jnp
from jax import lax
from jax.experimental import pallas as pl
from jax.experimental.pallas import tpu as pltpu
from jax.sharding import PartitionSpec as P

MESH = pl.DeviceIdType.MESH
LOOKAHEAD = 6
MOST_COLUMNS = 2816


def chunk_columns(depth):
    for columns in range(min(depth, MOST_COLUMNS) // 128 * 128, 0, -128):
        if depth % columns == 0:
            return columns
    return depth


def split(x):
    high = x.astype(jnp.bfloat16)
    low = (x - high.astype(jnp.float32)).astype(jnp.bfloat16)
    return jnp.concatenate([high, low], axis=0)


def kernel(n_occ, n_vir, columns, amp_hbm, slab_hbm, mirror_ref, out_ref, amp_buf, slab_buf, acc, part, by_occ, by_vir,
           amp_sem, slab_sem, occ_send, occ_recv, vir_send, vir_recv):
    occ, vir = lax.axis_index("occ"), lax.axis_index("vir")
    chunks = amp_buf.shape[0]
    rows, width = part.shape
    own_rows = rows // n_occ

    def copies(i):
        at = pl.ds(pl.multiple_of(i * columns, 128), columns)
        return (
            pltpu.make_async_copy(amp_hbm.at[:, at], amp_buf.at[i], amp_sem.at[i]),
            pltpu.make_async_copy(slab_hbm.at[:, at], slab_buf.at[i], slab_sem.at[i]),
        )

    ahead = min(LOOKAHEAD, chunks)
    for i in range(ahead):
        for copy in copies(i):
            copy.start()

    barrier = pltpu.get_barrier_semaphore()
    for d in range(1, n_occ):
        pl.semaphore_signal(barrier, inc=1, device_id=(lax.rem(occ + d, n_occ), vir), device_id_type=MESH)
    for d in range(1, n_vir):
        pl.semaphore_signal(barrier, inc=1, device_id=(occ, lax.rem(vir + d, n_vir)), device_id_type=MESH)

    acc[...] = jnp.zeros_like(acc)

    @pl.loop(0, chunks)
    def _(i):
        @pl.when(i + ahead < chunks)
        def _():
            for copy in copies(i + ahead):
                copy.start()

        for copy in copies(i):
            copy.wait()
        acc[...] += lax.dot_general(
            split(amp_buf[i]), split(slab_buf[i]), (((1,), (1,)), ((), ())), preferred_element_type=jnp.float32
        )

    part[...] = (acc[:rows, :width] + (acc[:rows, width:] + acc[rows:, :width])) + acc[rows:, width:]
    pl.semaphore_wait(barrier, n_occ + n_vir - 2)

    sends = []
    for d in range(1, n_occ):
        to = lax.rem(occ + d, n_occ)
        copy = pltpu.make_async_remote_copy(
            src_ref=part.at[pl.ds(pl.multiple_of(to * own_rows, 8), own_rows), :],
            dst_ref=by_occ.at[d - 1],
            send_sem=occ_send.at[d - 1],
            recv_sem=occ_recv.at[d - 1],
            device_id=(to, vir),
            device_id_type=MESH,
        )
        copy.start()
        sends.append(copy)
    total = part[pl.ds(pl.multiple_of(occ * own_rows, 8), own_rows), :]
    for d in range(1, n_occ):
        sends[d - 1].wait_recv()
        total = total + by_occ[d - 1]
    by_vir[vir] = total

    for d in range(1, n_vir):
        copy = pltpu.make_async_remote_copy(
            src_ref=by_vir.at[vir],
            dst_ref=by_vir.at[vir],
            send_sem=vir_send.at[d - 1],
            recv_sem=vir_recv.at[vir],
            device_id=(occ, lax.rem(vir + d, n_vir)),
            device_id_type=MESH,
        )
        copy.start()
        sends.append(copy)
    for d in range(1, n_vir):
        source = lax.rem(vir + d, n_vir)
        pltpu.make_async_remote_copy(
            src_ref=by_vir.at[source],
            dst_ref=by_vir.at[source],
            send_sem=vir_send.at[d - 1],
            recv_sem=vir_recv.at[source],
            device_id=(occ, source),
            device_id_type=MESH,
        ).wait_recv()
    total = by_vir[0]
    for source in range(1, n_vir):
        total = total + by_vir[source]
    index = jnp.broadcast_to(mirror_ref[...], total.shape)
    out_ref[...] = total - jnp.take_along_axis(total, index, axis=1)
    for copy in sends:
        copy.wait_send()


def per_device(amplitudes, slab, mirror):
    n_occ, n_vir = lax.axis_size("occ"), lax.axis_size("vir")
    rows, depth = amplitudes.shape
    width = slab.shape[0]
    own_rows = rows // n_occ
    columns = chunk_columns(depth)
    chunks = depth // columns
    return pl.pallas_call(
        functools.partial(kernel, n_occ, n_vir, columns),
        out_shape=jax.ShapeDtypeStruct((own_rows, width), jnp.float32),
        in_specs=[
            pl.BlockSpec(memory_space=pltpu.MemorySpace.HBM),
            pl.BlockSpec(memory_space=pltpu.MemorySpace.HBM),
            pl.BlockSpec(memory_space=pltpu.VMEM),
        ],
        out_specs=pl.BlockSpec(memory_space=pltpu.VMEM),
        scratch_shapes=[
            pltpu.VMEM((chunks, rows, columns), jnp.float32),
            pltpu.VMEM((chunks, width, columns), jnp.float32),
            pltpu.VMEM((2 * rows, 2 * width), jnp.float32),
            pltpu.VMEM((rows, width), jnp.float32),
            pltpu.VMEM((n_occ - 1, own_rows, width), jnp.float32),
            pltpu.VMEM((n_vir, own_rows, width), jnp.float32),
            pltpu.SemaphoreType.DMA((chunks,)),
            pltpu.SemaphoreType.DMA((chunks,)),
            pltpu.SemaphoreType.DMA((n_occ - 1,)),
            pltpu.SemaphoreType.DMA((n_occ - 1,)),
            pltpu.SemaphoreType.DMA((n_vir - 1,)),
            pltpu.SemaphoreType.DMA((n_vir,)),
        ],
        compiler_params=pltpu.CompilerParams(
            collective_id=0, has_side_effects=True, vmem_limit_bytes=60 * 2**20
        ),
    )(amplitudes, slab, mirror.reshape(1, width))


def solution(mesh):
    placed = (P(None, ("occ", "vir")), P(None, ("occ", "vir")), P())
    return jax.shard_map(
        per_device, mesh=mesh, in_specs=placed, out_specs=P("occ", None), check_vma=False
    )
```

time: 71.7 us -> 26 us (0.36)
  blocking collectives: 42.1 us -> 0 us
  matrix products: 27.9 us -> 0 us
  Pallas kernels: 0 us -> 24.5 us
    psum x1 -> x0, blocking collectives: 42.1 us -> none  [per_device(): summed = lax.psum(partial_sum, ('occ', 'vir'))]
    dot_general x1 -> x0, matrix products: 27.9 us -> none  [contract(): lax.dot_general(left, right, (((1,), (1,)), ((), ())), precision=lax.Prec...]
    pallas_call x0 -> x1, Pallas kernels: none -> 24.5 us  [per_device(): pl.pallas_call(functools.partial(kernel, n_occ, n_vir, columns), out_shap...]
    unnamed x2 -> x1, local copies, waits for them, and re-layouts: 0.01 us -> 1.3 us
where the time goes in v1:
time: 26 us; the launch traced here: 25.8 us
  Pallas kernels  24.5 us (94%)
  local copies, waits for them, and re-layouts  1.3 us (5%)
    pallas_call x1, Pallas kernels, per_device(): pl.pallas_call(functools.partial(kernel, n_occ, n_vir, columns), out_shap...  24.5 us
    unnamed x1, local copies, waits for them, and re-layouts  1.3 us

profile of v1, /device:TPU:0, one launch (start us, length us, event | category | flops | bytes accessed | tf_op | source)
XLA Modules:
  0.0 25.8 jit_solution(7767754999849929126)
XLA Ops:
  0.0 24.5 %shard_map.37 = f32[16,128]{1,0:T(8,128)} custom-call(f32[64,45056]{1,0:T(8,128)} %amp_hbm.1, f32[128,45056]{1,0:T(8,128)} %slab_hbm.1, s32[1,128]{1,0:T(1,128)} %bitcast.1), custom_call_target="tpu_custom_call" | custom-call | tf_op jit(solution)/shard_map/pallas_call | solution.py:127
  24.5 1.3 %copy.5 = f32[16,128]{1,0:T(8,128)} copy(f32[16,128]{1,0:T(8,128)} %shard_map.37) | data formatting | bytes 16384

commit v2 on v1

--- a/solution.py
+++ b/solution.py
@@ -25,12 +25,21 @@
     return jnp.concatenate([high, low], axis=0)
 
 
-def kernel(n_occ, n_vir, columns, amp_hbm, slab_hbm, mirror_ref, out_ref, amp_buf, slab_buf, acc, part, by_occ, by_vir,
-           amp_sem, slab_sem, occ_send, occ_recv, vir_send, vir_recv):
+def kernel(n_occ, n_vir, columns, amp_hbm, slab_hbm, mirror_hbm, out_ref, amp_buf, slab_buf, mirror_buf, acc, part, by_rank,
+           by_vir, amp_sem, slab_sem, mirror_sem, rank_send, rank_recv, vir_send, vir_recv):
     occ, vir = lax.axis_index("occ"), lax.axis_index("vir")
     chunks = amp_buf.shape[0]
     rows, width = part.shape
-    own_rows = rows // n_occ
+    n_half = 2
+    half_rows = rows // n_occ // n_half
+    half = lax.rem(vir, n_half)
+    pair = vir - half
+    ranks = n_occ * n_half
+    rank = occ * n_half + half
+
+    def ranked(d):
+        other = lax.rem(rank + d, ranks)
+        return other, (other // n_half, pair + lax.rem(other, n_half))
 
     def copies(i):
         at = pl.ds(pl.multiple_of(i * columns, 128), columns)
@@ -44,11 +53,14 @@
         for copy in copies(i):
             copy.start()
 
+    mirror_copy = pltpu.make_async_copy(mirror_hbm, mirror_buf, mirror_sem)
+    mirror_copy.start()
+
     barrier = pltpu.get_barrier_semaphore()
-    for d in range(1, n_occ):
-        pl.semaphore_signal(barrier, inc=1, device_id=(lax.rem(occ + d, n_occ), vir), device_id_type=MESH)
-    for d in range(1, n_vir):
-        pl.semaphore_signal(barrier, inc=1, device_id=(occ, lax.rem(vir + d, n_vir)), device_id_type=MESH)
+    for d in range(1, ranks):
+        pl.semaphore_signal(barrier, inc=1, device_id=ranked(d)[1], device_id_type=MESH)
+    for d in range(n_half, n_vir):
+        pl.semaphore_signal(barrier, inc=1, device_id=(occ, lax.rem(pair + d, n_vir)), device_id_type=MESH)
 
     acc[...] = jnp.zeros_like(acc)
 
@@ -66,25 +78,28 @@
         )
 
     part[...] = (acc[:rows, :width] + (acc[:rows, width:] + acc[rows:, :width])) + acc[rows:, width:]
-    pl.semaphore_wait(barrier, n_occ + n_vir - 2)
+    pl.semaphore_wait(barrier, ranks - 1 + n_vir - n_half)
+
+    def rows_of(other):
+        return part.at[pl.ds(pl.multiple_of(other * half_rows, 8), half_rows), :]
 
     sends = []
-    for d in range(1, n_occ):
-        to = lax.rem(occ + d, n_occ)
+    for d in range(1, ranks):
+        other, device = ranked(d)
         copy = pltpu.make_async_remote_copy(
-            src_ref=part.at[pl.ds(pl.multiple_of(to * own_rows, 8), own_rows), :],
-            dst_ref=by_occ.at[d - 1],
-            send_sem=occ_send.at[d - 1],
-            recv_sem=occ_recv.at[d - 1],
-            device_id=(to, vir),
+            src_ref=rows_of(other),
+            dst_ref=by_rank.at[d - 1],
+            send_sem=rank_send.at[d - 1],
+            recv_sem=rank_recv.at[d - 1],
+            device_id=device,
             device_id_type=MESH,
         )
         copy.start()
         sends.append(copy)
-    total = part[pl.ds(pl.multiple_of(occ * own_rows, 8), own_rows), :]
-    for d in range(1, n_occ):
+    total = rows_of(rank)[...]
+    for d in range(1, ranks):
         sends[d - 1].wait_recv()
-        total = total + by_occ[d - 1]
+        total = total + by_rank[d - 1]
     by_vir[vir] = total
 
     for d in range(1, n_vir):
@@ -108,11 +123,13 @@
             device_id=(occ, source),
             device_id_type=MESH,
         ).wait_recv()
-    total = by_vir[0]
-    for source in range(1, n_vir):
-        total = total + by_vir[source]
-    index = jnp.broadcast_to(mirror_ref[...], total.shape)
-    out_ref[...] = total - jnp.take_along_axis(total, index, axis=1)
+    mirror_copy.wait()
+    for h in range(n_half):
+        total = by_vir[h]
+        for source in range(h + n_half, n_vir, n_half):
+            total = total + by_vir[source]
+        index = jnp.broadcast_to(mirror_buf[...], total.shape)
+        out_ref[h * half_rows:(h + 1) * half_rows, :] = total - jnp.take_along_axis(total, index, axis=1)
     for copy in sends:
         copy.wait_send()
 
@@ -126,24 +143,26 @@
     chunks = depth // columns
     return pl.pallas_call(
         functools.partial(kernel, n_occ, n_vir, columns),
-        out_shape=jax.ShapeDtypeStruct((own_rows, width), jnp.float32),
+        out_shape=pltpu.VMEM((own_rows, width), jnp.float32),
         in_specs=[
             pl.BlockSpec(memory_space=pltpu.MemorySpace.HBM),
             pl.BlockSpec(memory_space=pltpu.MemorySpace.HBM),
-            pl.BlockSpec(memory_space=pltpu.VMEM),
+            pl.BlockSpec(memory_space=pltpu.MemorySpace.HBM),
         ],
         out_specs=pl.BlockSpec(memory_space=pltpu.VMEM),
         scratch_shapes=[
             pltpu.VMEM((chunks, rows, columns), jnp.float32),
             pltpu.VMEM((chunks, width, columns), jnp.float32),
+            pltpu.VMEM((1, width), jnp.int32),
             pltpu.VMEM((2 * rows, 2 * width), jnp.float32),
             pltpu.VMEM((rows, width), jnp.float32),
-            pltpu.VMEM((n_occ - 1, own_rows, width), jnp.float32),
-            pltpu.VMEM((n_vir, own_rows, width), jnp.float32),
+            pltpu.VMEM((2 * n_occ - 1, own_rows // 2, width), jnp.float32),
+            pltpu.VMEM((n_vir, own_rows // 2, width), jnp.float32),
             pltpu.SemaphoreType.DMA((chunks,)),
             pltpu.SemaphoreType.DMA((chunks,)),
-            pltpu.SemaphoreType.DMA((n_occ - 1,)),
-            pltpu.SemaphoreType.DMA((n_occ - 1,)),
+            pltpu.SemaphoreType.DMA(()),
+            pltpu.SemaphoreType.DMA((2 * n_occ - 1,)),
+            pltpu.SemaphoreType.DMA((2 * n_occ - 1,)),
             pltpu.SemaphoreType.DMA((n_vir - 1,)),
             pltpu.SemaphoreType.DMA((n_vir,)),
         ],

time: 26 us -> 24 us (0.923)
  Pallas kernels: 24.5 us -> 23.2 us
  local copies, waits for them, and re-layouts: 1.3 us -> 0.6 us
    pallas_call x1, Pallas kernels: 24.5 us -> 23.2 us  [per_device(): pl.pallas_call(functools.partial(kernel, n_occ, n_vir, columns), out_shap...]
    unnamed x1, local copies, waits for them, and re-layouts: 1.3 us -> 0.6 us
where the time goes in v2:
time: 24 us; the launch traced here: 23.9 us
  Pallas kernels  23.2 us (97%)
  local copies, waits for them, and re-layouts  0.6 us (2%)
    pallas_call x1, Pallas kernels, per_device(): pl.pallas_call(functools.partial(kernel, n_occ, n_vir, columns), out_shap...  23.2 us
    unnamed x1, local copies, waits for them, and re-layouts  0.6 us

profile of v2, /device:TPU:0, one launch (start us, length us, event | category | flops | bytes accessed | tf_op | source)
XLA Modules:
  0.0 23.9 jit_solution(18342206504267879848)
XLA Ops:
  0.0 23.2 %shard_map.37 = f32[16,128]{1,0:T(8,128)S(1)} custom-call(f32[64,45056]{1,0:T(8,128)} %amp_hbm.1, f32[128,45056]{1,0:T(8,128)} %slab_hbm.1, s32[1,128]{1,0:T(1,128)} %bitcast.1), custom_call_target="tpu_custom_call" | custom-call | tf_op jit(solution)/shard_map/pallas_call | solution.py:144
  23.3 0.6 %copy.5 = f32[16,128]{1,0:T(8,128)} copy(f32[16,128]{1,0:T(8,128)S(1)} %shard_map.37) | data formatting | bytes 16384

commit v3 on v2

--- a/solution.py
+++ b/solution.py
@@ -8,8 +8,8 @@
 from jax.sharding import PartitionSpec as P
 
 MESH = pl.DeviceIdType.MESH
-LOOKAHEAD = 6
-MOST_COLUMNS = 2816
+LOOKAHEAD = 4
+MOST_COLUMNS = 4096
 
 
 def chunk_columns(depth):

time: 24 us -> 24 us (level)
  no operation moved by 1% of the time
where the time goes in v3:
time: 24 us; the launch traced here: 23.9 us
  Pallas kernels  23.3 us (97%)
  local copies, waits for them, and re-layouts  0.6 us (2%)
    pallas_call x1, Pallas kernels, per_device(): pl.pallas_call(functools.partial(kernel, n_occ, n_vir, columns), out_shap...  23.3 us
    unnamed x1, local copies, waits for them, and re-layouts  0.6 us

profile of v3, /device:TPU:0, one launch (start us, length us, event | category | flops | bytes accessed | tf_op | source)
XLA Modules:
  0.0 23.9 jit_solution(11363319284862756638)
XLA Ops:
  0.0 23.3 %shard_map.37 = f32[16,128]{1,0:T(8,128)S(1)} custom-call(f32[64,45056]{1,0:T(8,128)} %amp_hbm.1, f32[128,45056]{1,0:T(8,128)} %slab_hbm.1, s32[1,128]{1,0:T(1,128)} %bitcast.1), custom_call_target="tpu_custom_call" | custom-call | tf_op jit(solution)/shard_map/pallas_call | solution.py:144
  23.3 0.6 %copy.5 = f32[16,128]{1,0:T(8,128)} copy(f32[16,128]{1,0:T(8,128)S(1)} %shard_map.37) | data formatting | bytes 16384
